TPU v7x, 32 devices: a whole 2x2x4 slice. The times are simulated.
32 devices in a mesh: groups: 2 (over x), tokens: 16 (over z, y, core).
Axes of the slice: x: 2, y: 2, z: 4, core: 2. Of those that a mesh axis runs over, the one named last changes fastest.
Arguments:
- text_query: bfloat16 [256, 2, 1280], P(('groups', 'tokens')), parts along dimension 0, may hold values from -6 to 6
- frame_key: bfloat16 [16384, 2, 1280], P(('groups', 'tokens')), parts along dimension 0, may hold values from -6 to 6
- frame_value: bfloat16 [16384, 2560], P(('groups', 'tokens')), parts along dimension 0, may hold values from -6 to 6
- forward_out: bfloat16 [256, 2, 2560], P(('groups', 'tokens')), parts along dimension 0, may hold values from -3 to 3
- out_grad: bfloat16 [256, 2560], P(('groups', 'tokens')), parts along dimension 0, may hold values from -1536 to 1536
- log_norms: float32 [256, 2, 10], P(('groups', 'tokens')), parts along dimension 0, as said below
- lambdas: float32 [10], replicated, may hold values from 0.2 to 0.8
- visits: int32 [32, 12], P('groups'), parts along dimension 0, may hold values from 0 to 15, all different within a row; in each aligned block of 16 rows (0 to 15, 16 to 31, ...) at most 14 rows name the same one
- bounds: int32 [32], P('groups'), parts along dimension 0, may hold values from 2 to 6, as said below
- text_count: int32 [1], replicated, may hold values from 64 to 128
Outputs:
- query_grad: bfloat16 [256, 2, 1280], P(('groups', 'tokens')), parts along dimension 0
- key_grad: bfloat16 [16384, 2, 1280], P(('groups', 'tokens')), parts along dimension 0
- value_grad: bfloat16 [16384, 2560], P(('groups', 'tokens')), parts along dimension 0
There are 2 independent parts, one for each index of `groups`. A program takes and returns all parts, laid end to end along the dimension named above; an argument that names none is the same for every part. Nothing has to cross between parts.
Inputs may be any that keep to these rules, and one draw needn't show every extreme that they name: `visits`: row b lists 6 frame shards for the first segment of text block b and then 6 for its second, all 12 different; every shard is listed by at most 14 blocks, a bound that some block reaches. Segment 1 of text block b begins at its row bounds[b]; some block has bounds 2 and some has 6, so no segment is longer than 6 rows. Text rows from text_count onward are padding in every group. `log_norms`: each entry lies within 1.5 of the logarithm of 3072.
All inputs are finite; a program needn't handle non-finite values.
Results may differ from a plain program's by a relative error of at most 0.005.
Values may be sent and summed in bfloat16 or wider, within the bound.
A program may use at most 128 MiB of HBM per device.

v0:
```python
import jax
import jax.numpy as jnp
from jax import lax
from jax.sharding import PartitionSpec as P


def segment_slots(in_first, in_second, bound_vals, block_ids, capacity, text_rows, text_count):
    start_row = jnp.where(in_second, bound_vals, 0)
    seg_length = jnp.where(in_first, bound_vals, jnp.where(in_second, text_rows - bound_vals, 0))
    slot_index = jnp.arange(capacity, dtype=jnp.int32)
    local_rows = start_row[:, None] + slot_index[None, :]
    global_rows = block_ids[:, None] * text_rows + local_rows
    used = jnp.logical_and(slot_index[None, :] < seg_length[:, None], global_rows < text_count[0])
    safe_rows = jnp.minimum(local_rows, text_rows - 1)
    return (safe_rows, used.astype(jnp.float32))


def place_rows(local_rows, used, text_rows):
    row_ids = jnp.arange(text_rows, dtype=jnp.int32)
    return (local_rows[:, :, None] == row_ids[None, None, :]).astype(jnp.float32) * used[:, :, None]


def visit_rows(
    query_rows,
    grad_rows,
    norm_rows,
    slope_rows,
    live_mask,
    frame_key,
    frame_value,
    lambdas,
    key_acc,
    value_acc,
):
    head_count = lambdas.shape[0]
    key_size = frame_key.shape[2] // head_count
    value_size = frame_value.shape[1] // head_count
    score_scale = float(key_size) ** (-0.5)
    part_rows = query_rows.shape[0]

    def head_step(head_index, running):
        key_total, value_total, query_part = running
        q_head = lax.dynamic_slice_in_dim(query_rows, head_index * key_size, key_size, 2)
        k_head = lax.dynamic_slice_in_dim(frame_key, head_index * key_size, key_size, 2)
        v_head = lax.dynamic_slice_in_dim(frame_value, head_index * value_size, value_size, 1)
        g_head = lax.dynamic_slice_in_dim(grad_rows, head_index * value_size, value_size, 1)
        norm_head = lax.dynamic_index_in_dim(norm_rows, head_index, 2, keepdims=False)
        slope_head = lax.dynamic_index_in_dim(slope_rows, head_index, 2, keepdims=False)
        weight_two = lax.dynamic_index_in_dim(lambdas, head_index, 0, keepdims=False)
        spread = jnp.dot(g_head, v_head.T, preferred_element_type=jnp.float32)
        score_one = (
            jnp.dot(q_head[:, 0], k_head[:, 0].T, preferred_element_type=jnp.float32) * score_scale
        )
        score_two = (
            jnp.dot(q_head[:, 1], k_head[:, 1].T, preferred_element_type=jnp.float32) * score_scale
        )
        prob_one = live_mask[:, None] * jnp.exp(score_one - norm_head[:, 0:1])
        prob_two = live_mask[:, None] * jnp.exp(score_two - norm_head[:, 1:2])
        grad_one = (prob_one * (spread - slope_head[:, 0:1])).astype(jnp.bfloat16)
        grad_two = (prob_two * (-weight_two * spread - slope_head[:, 1:2])).astype(jnp.bfloat16)
        mixed_weight = (prob_one - weight_two * prob_two).astype(jnp.bfloat16)
        value_new = jnp.dot(mixed_weight.T, g_head, preferred_element_type=jnp.float32)
        key_new = (
            jnp.stack(
                [
                    jnp.dot(grad_one.T, q_head[:, 0], preferred_element_type=jnp.float32),
                    jnp.dot(grad_two.T, q_head[:, 1], preferred_element_type=jnp.float32),
                ],
                axis=1,
            )
            * score_scale
        )
        query_new = (
            jnp.stack(
                [
                    jnp.dot(grad_one, k_head[:, 0], preferred_element_type=jnp.float32),
                    jnp.dot(grad_two, k_head[:, 1], preferred_element_type=jnp.float32),
                ],
                axis=1,
            )
            * score_scale
        )
        key_old = lax.dynamic_slice_in_dim(key_total, head_index * key_size, key_size, 2)
        key_total = lax.dynamic_update_slice_in_dim(
            key_total, key_old + key_new, head_index * key_size, 2
        )
        value_old = lax.dynamic_slice_in_dim(value_total, head_index * value_size, value_size, 1)
        value_total = lax.dynamic_update_slice_in_dim(
            value_total, value_old + value_new, head_index * value_size, 1
        )
        query_part = lax.dynamic_update_slice_in_dim(
            query_part, query_new, head_index * key_size, 2
        )
        return (key_total, value_total, query_part)

    query_start = jnp.zeros((part_rows,) + query_rows.shape[1:], jnp.float32)
    return lax.fori_loop(0, head_count, head_step, (key_acc, value_acc, query_start))


def per_device(
    text_query,
    frame_key,
    frame_value,
    forward_out,
    out_grad,
    log_norms,
    lambdas,
    visits,
    bounds,
    text_count,
):
    shard_count = lax.axis_size("tokens")
    my_index = lax.axis_index("tokens")
    text_rows = text_query.shape[0]
    head_count = lambdas.shape[0]
    value_size = frame_value.shape[1] // head_count
    visit_width = visits.shape[1] // 2
    capacity = 3 * text_rows // 4
    grads_wide = out_grad.astype(jnp.float32).reshape(text_rows, head_count, value_size)
    outs_wide = forward_out.astype(jnp.float32).reshape(text_rows, 2, head_count, value_size)
    map_coefs = jnp.stack([jnp.ones_like(lambdas), -lambdas])
    slopes = jnp.sum(grads_wide[:, None] * outs_wide, axis=3) * map_coefs[None]
    all_norms, all_slopes = (
        lax.all_gather(log_norms, "tokens", axis=0, tiled=True),
        lax.all_gather(slopes, "tokens", axis=0, tiled=True),
    )
    zero_keys = jnp.zeros(frame_key.shape, jnp.float32)
    zero_values = jnp.zeros(frame_value.shape, jnp.float32)
    shards = jnp.arange(shard_count, dtype=jnp.int32)
    query_shape = text_query.shape[1:]
    flat_width = query_shape[0] * query_shape[1]
    my_list = lax.dynamic_index_in_dim(visits, my_index, 0, keepdims=False)
    my_bound = lax.dynamic_index_in_dim(bounds, my_index, 0, keepdims=False)
    send_first = jnp.any(my_list[:visit_width][None, :] == shards[:, None], axis=1)
    send_second = jnp.any(my_list[visit_width:][None, :] == shards[:, None], axis=1)
    send_rows, send_used = segment_slots(
        send_first,
        send_second,
        jnp.broadcast_to(my_bound, (shard_count,)),
        jnp.broadcast_to(my_index, (shard_count,)),
        capacity,
        text_rows,
        text_count,
    )
    recv_first = jnp.any(visits[:, :visit_width] == my_index, axis=1)
    recv_second = jnp.any(visits[:, visit_width:] == my_index, axis=1)
    recv_rows, recv_used = segment_slots(
        recv_first, recv_second, bounds, shards, capacity, text_rows, text_count
    )
    flat_send = send_rows.reshape(-1)
    sent_query = jnp.take(text_query, flat_send, axis=0)
    sent_grad = jnp.take(out_grad, flat_send, axis=0)
    got_query, got_grad = (
        lax.all_to_all(sent_query, "tokens", split_axis=0, concat_axis=0, tiled=True),
        lax.all_to_all(sent_grad, "tokens", split_axis=0, concat_axis=0, tiled=True),
    )
    global_recv = (shards[:, None] * text_rows + recv_rows).reshape(-1)
    norm_rows = jnp.take(all_norms, global_recv, axis=0)
    slope_rows = jnp.take(all_slopes, global_recv, axis=0)
    key_acc, value_acc, query_part = visit_rows(
        got_query,
        got_grad,
        norm_rows,
        slope_rows,
        recv_used.reshape(-1),
        frame_key,
        frame_value,
        lambdas,
        zero_keys,
        zero_values,
    )
    came_back = lax.all_to_all(query_part, "tokens", split_axis=0, concat_axis=0, tiled=True)
    grouped = came_back.reshape(shard_count, came_back.shape[0] // shard_count, flat_width)
    placing = place_rows(send_rows, send_used, text_rows)
    query_sum = jnp.einsum(
        "jsx,jsc->xc", placing, grouped, precision=lax.Precision.HIGHEST
    ).reshape((text_rows,) + query_shape)
    return (
        query_sum.astype(jnp.bfloat16),
        key_acc.astype(jnp.bfloat16),
        value_acc.astype(jnp.bfloat16),
    )


def solution(mesh):
    return jax.shard_map(
        per_device,
        mesh=mesh,
        in_specs=(
            P(("groups", "tokens"), None, None),
            P(("groups", "tokens"), None, None),
            P(("groups", "tokens"), None),
            P(("groups", "tokens"), None, None),
            P(("groups", "tokens"), None),
            P(("groups", "tokens"), None, None),
            P(),
            P("groups", None),
            P("groups"),
            P(),
        ),
        out_specs=(
            P(("groups", "tokens"), None, None),
            P(("groups", "tokens"), None, None),
            P(("groups", "tokens"), None),
        ),
        check_vma=False,
    )
```

profile of v0, /device:TPU:9, one launch (start us, length us, event | category | flops | bytes accessed | tf_op | source)
XLA Modules:
  0.0 243.4 jit_solution(16591408216141167793)
XLA Ops:
  5.0 2.1 gather_fusion.1
  8.4 6.6 %all-to-all-start.1 = ((bf16[16,6,2560]{2,1,0:T(8,128)(2,1)}), bf16[16,6,2560]{2,1,0:T(8,128)(2,1)S(1)}, u32[]{:S(2)}, u32[]{:S(2)}) async-start(bf16[16,6,2560]{2,1,0:T(8,128)(2,1)} %broadcast_select_fusion.1), calls=%async_computation.1 | async-start | bytes 1310720 | tf_op jit(solution)/shard_map/all_to_all | solution.py:155
  18.7 13.2 %all-to-all-done.1 = bf16[16,6,2560]{2,1,0:T(8,128)(2,1)S(1)} async-done(((bf16[16,6,2560]{2,1,0:T(8,128)(2,1)}), bf16[16,6,2560]{2,1,0:T(8,128)(2,1)S(1)}, u32[]{:S(2)}, u32[]{:S(2)}) %all-to-all-start.1) | async-done | bytes 491552 | tf_op jit(solution)/shard_map/all_to_all | solution.py:155
  31.9 4.5 %all-to-all-start = ((bf16[96,2,1280]{2,1,0:T(2,128)(2,1)}), bf16[96,2,1280]{2,1,0:T(2,128)(2,1)S(1)}, u32[]{:S(2)}, u32[]{:S(2)}) async-start(bf16[96,2,1280]{2,1,0:T(2,128)(2,1)} %broadcast_select_fusion), calls=%async_computation | async-start | bytes 983040 | tf_op jit(solution)/shard_map/all_to_all | solution.py:154
  36.4 23.7 %all_gather.6 = f32[128,2,10]{2,1,0:T(2,128)S(1)} all-gather(f32[8,2,10]{2,1,0:T(2,128)S(1)} %copy-done.4), channel_id=1, replica_groups=mesh['groups'=2,'tokens'=16] {'tokens'}, dimensions={0}, use_global_device_ids=true | all-gather | bytes 10880 | tf_op jit(solution)/shard_map/all_gather | solution.py:124
  60.8 17.2 %all_gather.7 = f32[128,2,10]{2,1,0:T(2,128)S(1)} all-gather(f32[8,2,10]{2,1,0:T(2,128)S(1)} %copy.61), channel_id=1, replica_groups=mesh['groups'=2,'tokens'=16] {'tokens'}, dimensions={0}, use_global_device_ids=true | all-gather | bytes 10880 | tf_op jit(solution)/shard_map/all_gather | solution.py:125
  80.5 3.0 %broadcast_in_dim.72 = f32[512,2560]{1,0:T(8,128)} broadcast(f32[]{:T(128)} %constant.125.clone.1), dimensions={} | broadcast | bytes 5242884 | tf_op jit(solution)/shard_map/broadcast_in_dim | solution.py:128
  83.5 3.6 %broadcast_in_dim.71.clone = f32[512,2,1280]{2,1,0:T(2,128)} broadcast(f32[]{:T(128)} %constant.125.clone.1), dimensions={} | broadcast | bytes 5242884 | tf_op jit(solution)/shard_map/broadcast_in_dim | solution.py:127
  87.1 122.9 %while.18 = (s32[]{:T(128)}, f32[512,2,1280]{2,1,0:T(2,128)}, f32[512,2560]{1,0:T(8,128)}, f32[96,2,1280]{2,1,0:T(2,128)}, bf16[96,2,1280]{2,1,0:T(2,128)(2,1)S(...) while((s32[]{:T(128)}, f32[512,2,1280]{2,1,0:T(2,128)}, ...), condition=%wide.region_6.8_spmd.clone, body=%wide.region_5.7_spmd.clone.sunk | while | flops 127189576 | bytes 9318833 | solution.py:97
  90.5 1.6 constant_dynamic-slice_fusion.11
  96.5 2.8 %fusion.66 = f32[512,2560]{1,0:T(8,128)} fusion(f32[512,2560]{1,0:T(8,128)} %get-tuple-element.518, s32[]{:T(128)S(6)} %select_n.149, f32[96,512]{1,0:T(8,128)S(1)} %get-tuple-element.493, f32[96,512]{1,0:T(8,128)S(1)} %fusion.64, f32[]{:T(128)} %bitcast.109, bf16[96,2560]{1,0:T(8,128)(2,1)S(1)} %get-tuple-element.545), kind=kOutput, calls=%fused_computation.6.clone.1 | convolution fusion | flops 25444352 | bytes 1492480 | tf_op jit(solution)/shard_map/while/body/eval_jaxpr/dot_general | solution.py:62
  102.7 1.6 constant_dynamic-slice_fusion.11
  108.8 2.9 %fusion.66 = f32[512,2560]{1,0:T(8,128)} fusion(f32[512,2560]{1,0:T(8,128)} %get-tuple-element.518, s32[]{:T(128)S(6)} %select_n.149, f32[96,512]{1,0:T(8,128)S(1)} %get-tuple-element.493, f32[96,512]{1,0:T(8,128)S(1)} %fusion.64, f32[]{:T(128)} %bitcast.109, bf16[96,2560]{1,0:T(8,128)(2,1)S(1)} %get-tuple-element.545), kind=kOutput, calls=%fused_computation.6.clone.1 | convolution fusion | flops 25444352 | bytes 1492480 | tf_op jit(solution)/shard_map/while/body/eval_jaxpr/dot_general | solution.py:62
  115.1 1.7 constant_dynamic-slice_fusion.11
  121.2 2.8 %fusion.66 = f32[512,2560]{1,0:T(8,128)} fusion(f32[512,2560]{1,0:T(8,128)} %get-tuple-element.518, s32[]{:T(128)S(6)} %select_n.149, f32[96,512]{1,0:T(8,128)S(1)} %get-tuple-element.493, f32[96,512]{1,0:T(8,128)S(1)} %fusion.64, f32[]{:T(128)} %bitcast.109, bf16[96,2560]{1,0:T(8,128)(2,1)S(1)} %get-tuple-element.545), kind=kOutput, calls=%fused_computation.6.clone.1 | convolution fusion | flops 25444352 | bytes 1492480 | tf_op jit(solution)/shard_map/while/body/eval_jaxpr/dot_general | solution.py:62
  127.3 1.7 constant_dynamic-slice_fusion.11
  133.5 2.8 %fusion.66 = f32[512,2560]{1,0:T(8,128)} fusion(f32[512,2560]{1,0:T(8,128)} %get-tuple-element.518, s32[]{:T(128)S(6)} %select_n.149, f32[96,512]{1,0:T(8,128)S(1)} %get-tuple-element.493, f32[96,512]{1,0:T(8,128)S(1)} %fusion.64, f32[]{:T(128)} %bitcast.109, bf16[96,2560]{1,0:T(8,128)(2,1)S(1)} %get-tuple-element.545), kind=kOutput, calls=%fused_computation.6.clone.1 | convolution fusion | flops 25444352 | bytes 1492480 | tf_op jit(solution)/shard_map/while/body/eval_jaxpr/dot_general | solution.py:62
  139.7 1.6 constant_dynamic-slice_fusion.11
  145.7 2.8 %fusion.66 = f32[512,2560]{1,0:T(8,128)} fusion(f32[512,2560]{1,0:T(8,128)} %get-tuple-element.518, s32[]{:T(128)S(6)} %select_n.149, f32[96,512]{1,0:T(8,128)S(1)} %get-tuple-element.493, f32[96,512]{1,0:T(8,128)S(1)} %fusion.64, f32[]{:T(128)} %bitcast.109, bf16[96,2560]{1,0:T(8,128)(2,1)S(1)} %get-tuple-element.545), kind=kOutput, calls=%fused_computation.6.clone.1 | convolution fusion | flops 25444352 | bytes 1492480 | tf_op jit(solution)/shard_map/while/body/eval_jaxpr/dot_general | solution.py:62
  151.9 1.7 constant_dynamic-slice_fusion.11
  158.1 2.8 %fusion.66 = f32[512,2560]{1,0:T(8,128)} fusion(f32[512,2560]{1,0:T(8,128)} %get-tuple-element.518, s32[]{:T(128)S(6)} %select_n.149, f32[96,512]{1,0:T(8,128)S(1)} %get-tuple-element.493, f32[96,512]{1,0:T(8,128)S(1)} %fusion.64, f32[]{:T(128)} %bitcast.109, bf16[96,2560]{1,0:T(8,128)(2,1)S(1)} %get-tuple-element.545), kind=kOutput, calls=%fused_computation.6.clone.1 | convolution fusion | flops 25444352 | bytes 1492480 | tf_op jit(solution)/shard_map/while/body/eval_jaxpr/dot_general | solution.py:62
  164.3 1.7 constant_dynamic-slice_fusion.11
  170.4 2.8 %fusion.66 = f32[512,2560]{1,0:T(8,128)} fusion(f32[512,2560]{1,0:T(8,128)} %get-tuple-element.518, s32[]{:T(128)S(6)} %select_n.149, f32[96,512]{1,0:T(8,128)S(1)} %get-tuple-element.493, f32[96,512]{1,0:T(8,128)S(1)} %fusion.64, f32[]{:T(128)} %bitcast.109, bf16[96,2560]{1,0:T(8,128)(2,1)S(1)} %get-tuple-element.545), kind=kOutput, calls=%fused_computation.6.clone.1 | convolution fusion | flops 25444352 | bytes 1492480 | tf_op jit(solution)/shard_map/while/body/eval_jaxpr/dot_general | solution.py:62
  176.6 1.7 constant_dynamic-slice_fusion.11
  182.7 2.8 %fusion.66 = f32[512,2560]{1,0:T(8,128)} fusion(f32[512,2560]{1,0:T(8,128)} %get-tuple-element.518, s32[]{:T(128)S(6)} %select_n.149, f32[96,512]{1,0:T(8,128)S(1)} %get-tuple-element.493, f32[96,512]{1,0:T(8,128)S(1)} %fusion.64, f32[]{:T(128)} %bitcast.109, bf16[96,2560]{1,0:T(8,128)(2,1)S(1)} %get-tuple-element.545), kind=kOutput, calls=%fused_computation.6.clone.1 | convolution fusion | flops 25444352 | bytes 1492480 | tf_op jit(solution)/shard_map/while/body/eval_jaxpr/dot_general | solution.py:62
  188.9 1.7 constant_dynamic-slice_fusion.11
  195.0 2.8 %fusion.66 = f32[512,2560]{1,0:T(8,128)} fusion(f32[512,2560]{1,0:T(8,128)} %get-tuple-element.518, s32[]{:T(128)S(6)} %select_n.149, f32[96,512]{1,0:T(8,128)S(1)} %get-tuple-element.493, f32[96,512]{1,0:T(8,128)S(1)} %fusion.64, f32[]{:T(128)} %bitcast.109, bf16[96,2560]{1,0:T(8,128)(2,1)S(1)} %get-tuple-element.545), kind=kOutput, calls=%fused_computation.6.clone.1 | convolution fusion | flops 25444352 | bytes 1492480 | tf_op jit(solution)/shard_map/while/body/eval_jaxpr/dot_general | solution.py:62
  207.2 2.8 %fusion.66 = f32[512,2560]{1,0:T(8,128)} fusion(f32[512,2560]{1,0:T(8,128)} %get-tuple-element.518, s32[]{:T(128)S(6)} %select_n.149, f32[96,512]{1,0:T(8,128)S(1)} %get-tuple-element.493, f32[96,512]{1,0:T(8,128)S(1)} %fusion.64, f32[]{:T(128)} %bitcast.109, bf16[96,2560]{1,0:T(8,128)(2,1)S(1)} %get-tuple-element.545), kind=kOutput, calls=%fused_computation.6.clone.1 | convolution fusion | flops 25444352 | bytes 1492480 | tf_op jit(solution)/shard_map/while/body/eval_jaxpr/dot_general | solution.py:62
  210.0 6.6 %all-to-all-start.2 = ((f32[96,2,1280]{2,1,0:T(2,128)}), f32[96,2,1280]{2,1,0:T(2,128)S(1)}, u32[]{:S(2)}, u32[]{:S(2)}) async-start(f32[96,2,1280]{2,1,0:T(2,128)} %get-tuple-element.205), calls=%async_computation.2 | async-start | bytes 1966080 | tf_op jit(solution)/shard_map/all_to_all | solution.py:172
  216.8 5.9 %convert_element_type.46 = bf16[512,2,1280]{2,1,0:T(2,128)(2,1)} convert(f32[512,2,1280]{2,1,0:T(2,128)} %get-tuple-element.206) | non-fusion elementwise | flops 1310720 | bytes 7864320 | tf_op jit(solution)/shard_map/convert_element_type | solution.py:180
  222.7 1.8 convert_element_type.47
  224.5 15.7 %all-to-all-done.2 = f32[96,2,1280]{2,1,0:T(2,128)S(1)} async-done(((f32[96,2,1280]{2,1,0:T(2,128)}), f32[96,2,1280]{2,1,0:T(2,128)S(1)}, u32[]{:S(2)}, u32[]{:S(2)}) %all-to-all-start.2) | async-done | bytes 983072 | tf_op jit(solution)/shard_map/all_to_all | solution.py:172
  (255 shorter events, 86.5 us)
Async XLA Ops:
  0.6 15.0 %copy-start = (bf16[8,2,1280]{2,1,0:T(2,128)(2,1)S(1)}, bf16[8,2,1280]{2,1,0:T(2,128)(2,1)}, u32[]{:S(2)}) copy-start(bf16[8,2,1280]{2,1,0:T(2,128)(2,1)} %param.14) | copy-start | bytes 122884
  0.6 14.6 %copy-start.5 = (s32[16]{0:T(128)S(1)}, s32[16]{0:T(128)}, u32[]{:S(2)}) copy-start(s32[16]{0:T(128)} %param.22) | copy-start | bytes 196
  0.7 14.4 %copy-start.3 = (s32[16,12]{1,0:T(8,128)S(1)}, s32[16,12]{1,0:T(8,128)}, u32[]{:S(2)}) copy-start(s32[16,12]{1,0:T(8,128)} %param.21) | copy-start | bytes 2308
  0.7 14.8 %copy-start.1 = (bf16[8,2560]{1,0:T(8,128)(2,1)S(1)}, bf16[8,2560]{1,0:T(8,128)(2,1)}, u32[]{:S(2)}) copy-start(bf16[8,2560]{1,0:T(8,128)(2,1)} %param.18) | copy-start | bytes 122884
  0.7 14.6 %copy-start.6 = (f32[10]{0:T(128)S(1)}, f32[10]{0:T(128)}, u32[]{:S(2)}) copy-start(f32[10]{0:T(128)} %param.20) | copy-start | bytes 124
  0.7 14.8 %copy-start.2 = (bf16[8,2,2560]{2,1,0:T(2,128)(2,1)S(1)}, bf16[8,2,2560]{2,1,0:T(2,128)(2,1)}, u32[]{:S(2)}) copy-start(bf16[8,2,2560]{2,1,0:T(2,128)(2,1)} %param.17) | copy-start | bytes 245764
  5.0 31.4 %copy-start.4 = (f32[8,2,10]{2,1,0:T(2,128)S(1)}, f32[8,2,10]{2,1,0:T(2,128)}, u32[]{:S(2)}) copy-start(f32[8,2,10]{2,1,0:T(2,128)} %param.19) | copy-start | bytes 1924
  8.4 23.5 %all-to-all-start.1 = ((bf16[16,6,2560]{2,1,0:T(8,128)(2,1)}), bf16[16,6,2560]{2,1,0:T(8,128)(2,1)S(1)}, u32[]{:S(2)}, u32[]{:S(2)}) async-start(bf16[16,6,2560]{2,1,0:T(8,128)(2,1)} %broadcast_select_fusion.1), calls=%async_computation.1 | async-start | bytes 1310720 | tf_op jit(solution)/shard_map/all_to_all | solution.py:155
  31.9 47.4 %all-to-all-start = ((bf16[96,2,1280]{2,1,0:T(2,128)(2,1)}), bf16[96,2,1280]{2,1,0:T(2,128)(2,1)S(1)}, u32[]{:S(2)}, u32[]{:S(2)}) async-start(bf16[96,2,1280]{2,1,0:T(2,128)(2,1)} %broadcast_select_fusion), calls=%async_computation | async-start | bytes 983040 | tf_op jit(solution)/shard_map/all_to_all | solution.py:154
  210.0 12.7 %slice-start = ((s8[5242880]{0:T(1024)(128)(4,1)}), s8[1048576]{0:T(1024)(128)(4,1)S(1)}, s32[]{:S(2)}) async-start(s8[5242880]{0:T(1024)(128)(4,1)} %bitcast.112), calls=%async_computation.3 | async-start | bytes 2097152
  210.0 30.2 %all-to-all-start.2 = ((f32[96,2,1280]{2,1,0:T(2,128)}), f32[96,2,1280]{2,1,0:T(2,128)S(1)}, u32[]{:S(2)}, u32[]{:S(2)}) async-start(f32[96,2,1280]{2,1,0:T(2,128)} %get-tuple-element.205), calls=%async_computation.2 | async-start | bytes 1966080 | tf_op jit(solution)/shard_map/all_to_all | solution.py:172
  216.8 5.9 %slice-start.1 = ((s8[5242880]{0:T(1024)(128)(4,1)}), s8[4194304]{0:T(1024)(128)(4,1)S(1)}, s32[]{:S(2)}) async-start(s8[5242880]{0:T(1024)(128)(4,1)} %bitcast.112), calls=%async_computation.4 | async-start | bytes 8388608
where the time goes:
time: 246 us; the launch traced here: 243 us
  local copies, waits for them, and re-layouts  74.1 us (30%)
  matrix products  52.4 us (21%)
  blocking collectives  40.9 us (17%)
  waiting for transfers between devices  28.9 us (12%)
  other arithmetic  19.5 us (8%)
  starting transfers between devices  17.7 us (7%)
  loops' own time  7.6 us (3%)
    dot_general x10, matrix products, head_step(): jnp.dot(mixed_weight.T, g_head, preferred_element_type=jnp.float32)  28 us
    all_gather x1, blocking collectives, per_device(): lax.all_gather(log_norms, 'tokens', axis=0, tiled=True)  23.7 us
    all_gather x1, blocking collectives, per_device(): lax.all_gather(slopes, 'tokens', axis=0, tiled=True)  17.2 us
    slice x10, local copies, waits for them, and re-layouts, head_step(): k_head[:, 0]  16.7 us
    all_to_all x1, waiting for transfers between devices, per_device(): lax.all_to_all(query_part, 'tokens', split_axis=0, concat_axis=0, tiled=T...  15.7 us
    all_to_all x1, waiting for transfers between devices, per_device(): lax.all_to_all(sent_grad, 'tokens', split_axis=0, concat_axis=0, tiled=True)  13.2 us
    dynamic_update_slice x10, local copies, waits for them, and re-layouts, head_step(): lax.dynamic_update_slice_in_dim(key_total, key_old + key_new, head_index...  12.7 us
    dot_general x10, matrix products, head_step(): spread = jnp.dot(g_head, v_head.T, preferred_element_type=jnp.float32)  11.6 us
  transfers between devices with their start and end apart: 3, of which 2 were waited for; matrix products, arithmetic and copies ran while one was open for 5% of the time, Pallas kernels for 0%

commit v1 on v0

--- a/solution.py
+++ b/solution.py
@@ -2,6 +2,18 @@
 import jax.numpy as jnp
 from jax import lax
 from jax.sharding import PartitionSpec as P
+
+
+def gather_by_bits(array, axis, dim):
+    ways, here = (lax.axis_size(axis), lax.axis_index(axis))
+    grown, reach = (array, 1)
+    while reach < ways:
+        theirs = lax.ppermute(grown, axis, [(d, d ^ reach) for d in range(ways)])
+        mine_first = jnp.concatenate([grown, theirs], axis=dim)
+        theirs_first = jnp.concatenate([theirs, grown], axis=dim)
+        grown = jnp.where(here & reach == 0, mine_first, theirs_first)
+        reach = 2 * reach
+    return grown
 
 
 def segment_slots(in_first, in_second, bound_vals, block_ids, capacity, text_rows, text_count):
@@ -121,7 +133,7 @@
     map_coefs = jnp.stack([jnp.ones_like(lambdas), -lambdas])
     slopes = jnp.sum(grads_wide[:, None] * outs_wide, axis=3) * map_coefs[None]
     all_norms, all_slopes = (
-        lax.all_gather(log_norms, "tokens", axis=0, tiled=True),
+        gather_by_bits(log_norms, "tokens", 0),
         lax.all_gather(slopes, "tokens", axis=0, tiled=True),
     )
     zero_keys = jnp.zeros(frame_key.shape, jnp.float32)

time: 246 us -> 228 us (0.927)
  blocking collectives: 40.9 us -> 21.8 us
    all_gather x1 -> x0, blocking collectives: 23.7 us -> none  [per_device(): lax.all_gather(log_norms, 'tokens', axis=0, tiled=True)]
    all_gather x1, blocking collectives: 17.2 us -> 21.8 us  [per_device(): lax.all_gather(slopes, 'tokens', axis=0, tiled=True)]
    ppermute x0 -> x4, starting transfers between devices: none -> 4.15 us  [gather_by_bits(): theirs = lax.ppermute(grown, axis, [(d, d ^ reach) for d in range(ways)])]
    all_to_all x1, waiting for transfers between devices: 13.2 us -> 9.69 us  [per_device(): lax.all_to_all(sent_grad, 'tokens', split_axis=0, concat_axis=0, tiled=True)]
  transfers between devices with their start and end apart: 3 -> 7, of which waited for: 2 -> 3; matrix products, arithmetic and copies ran while one was open for 5% -> 9% of each run, Pallas kernels for 0% -> 0%
where the time goes in v1:
time: 228 us; the launch traced here: 226 us
  local copies, waits for them, and re-layouts  75.3 us (33%)
  matrix products  52.4 us (23%)
  waiting for transfers between devices  27.3 us (12%)
  blocking collectives  21.8 us (10%)
  other arithmetic  19.9 us (9%)
  starting transfers between devices  19.3 us (8%)
  loops' own time  7.61 us (3%)
    dot_general x10, matrix products, head_step(): jnp.dot(mixed_weight.T, g_head, preferred_element_type=jnp.float32)  28.1 us
    all_gather x1, blocking collectives, per_device(): lax.all_gather(slopes, 'tokens', axis=0, tiled=True)  21.8 us
    slice x10, local copies, waits for them, and re-layouts, head_step(): k_head[:, 0]  16.7 us
    all_to_all x1, waiting for transfers between devices, per_device(): lax.all_to_all(query_part, 'tokens', split_axis=0, concat_axis=0, tiled=T...  15.7 us
    dynamic_update_slice x10, local copies, waits for them, and re-layouts, head_step(): lax.dynamic_update_slice_in_dim(key_total, key_old + key_new, head_index...  12.7 us
    dot_general x10, matrix products, head_step(): spread = jnp.dot(g_head, v_head.T, preferred_element_type=jnp.float32)  11.6 us
    dynamic_slice x10, local copies, waits for them, and re-layouts, head_step(): lax.dynamic_slice_in_dim(key_total, head_index * key_size, key_size, 2)  10.8 us
    all_to_all x1, waiting for transfers between devices, per_device(): lax.all_to_all(sent_grad, 'tokens', split_axis=0, concat_axis=0, tiled=True)  9.69 us
  transfers between devices with their start and end apart: 7, of which 3 were waited for; matrix products, arithmetic and copies ran while one was open for 9% of the time, Pallas kernels for 0%

profile of v1, /device:TPU:9, one launch (start us, length us, event | category | flops | bytes accessed | tf_op | source)
XLA Modules:
  0.0 225.9 jit_solution(8189305380275012512)
XLA Ops:
  6.5 2.1 gather_fusion.1
  9.9 6.0 %all-to-all-start.1 = ((bf16[16,6,2560]{2,1,0:T(8,128)(2,1)}), bf16[16,6,2560]{2,1,0:T(8,128)(2,1)S(1)}, u32[]{:S(2)}, u32[]{:S(2)}) async-start(bf16[16,6,2560]{2,1,0:T(8,128)(2,1)} %broadcast_select_fusion.1), calls=%async_computation.1 | async-start | bytes 1310720 | tf_op jit(solution)/shard_map/all_to_all | solution.py:167
  21.0 2.0 collective-permute-done.1
  23.1 9.7 %all-to-all-done.1 = bf16[16,6,2560]{2,1,0:T(8,128)(2,1)S(1)} async-done(((bf16[16,6,2560]{2,1,0:T(8,128)(2,1)}), bf16[16,6,2560]{2,1,0:T(8,128)(2,1)S(1)}, u32[]{:S(2)}, u32[]{:S(2)}) %all-to-all-start.1) | async-done | bytes 491552 | tf_op jit(solution)/shard_map/all_to_all | solution.py:167
  32.8 4.5 %all-to-all-start = ((bf16[96,2,1280]{2,1,0:T(2,128)(2,1)}), bf16[96,2,1280]{2,1,0:T(2,128)(2,1)S(1)}, u32[]{:S(2)}, u32[]{:S(2)}) async-start(bf16[96,2,1280]{2,1,0:T(2,128)(2,1)} %broadcast_select_fusion), calls=%async_computation | async-start | bytes 983040 | tf_op jit(solution)/shard_map/all_to_all | solution.py:166
  37.4 2.2 collective-permute-start.3
  39.6 21.8 %all_gather.3 = f32[128,2,10]{2,1,0:T(2,128)S(1)} all-gather(f32[8,2,10]{2,1,0:T(2,128)S(1)} %copy.71), channel_id=1, replica_groups=mesh['groups'=2,'tokens'=16] {'tokens'}, dimensions={0}, use_global_device_ids=true | all-gather | bytes 10880 | tf_op jit(solution)/shard_map/all_gather | solution.py:137
  65.0 3.0 %broadcast_in_dim.72 = f32[512,2560]{1,0:T(8,128)} broadcast(f32[]{:T(128)} %constant.129.clone.1), dimensions={} | broadcast | bytes 5242884 | tf_op jit(solution)/shard_map/broadcast_in_dim | solution.py:140
  68.0 3.7 %broadcast_in_dim.71.clone = f32[512,2,1280]{2,1,0:T(2,128)} broadcast(f32[]{:T(128)} %constant.129.clone.1), dimensions={} | broadcast | bytes 5242884 | tf_op jit(solution)/shard_map/broadcast_in_dim | solution.py:139
  71.6 122.9 %while.18 = (s32[]{:T(128)}, f32[512,2,1280]{2,1,0:T(2,128)}, f32[512,2560]{1,0:T(8,128)}, f32[96,2,1280]{2,1,0:T(2,128)}, bf16[96,2,1280]{2,1,0:T(2,128)(2,1)S(...) while((s32[]{:T(128)}, f32[512,2,1280]{2,1,0:T(2,128)}, ...), condition=%wide.region_6.8_spmd.clone, body=%wide.region_5.7_spmd.clone.sunk | while | flops 127189576 | bytes 9318833 | solution.py:109
  75.0 1.6 constant_dynamic-slice_fusion.11
  81.1 2.8 %fusion.66 = f32[512,2560]{1,0:T(8,128)} fusion(f32[512,2560]{1,0:T(8,128)} %get-tuple-element.520, s32[]{:T(128)S(6)} %select_n.197, f32[96,512]{1,0:T(8,128)S(1)} %get-tuple-element.495, f32[96,512]{1,0:T(8,128)S(1)} %fusion.64, f32[]{:T(128)} %bitcast.112, bf16[96,2560]{1,0:T(8,128)(2,1)S(1)} %get-tuple-element.547), kind=kOutput, calls=%fused_computation.6.clone.1 | convolution fusion | flops 25444352 | bytes 1492480 | tf_op jit(solution)/shard_map/while/body/eval_jaxpr/dot_general | solution.py:74
  93.3 2.8 %fusion.66 = f32[512,2560]{1,0:T(8,128)} fusion(f32[512,2560]{1,0:T(8,128)} %get-tuple-element.520, s32[]{:T(128)S(6)} %select_n.197, f32[96,512]{1,0:T(8,128)S(1)} %get-tuple-element.495, f32[96,512]{1,0:T(8,128)S(1)} %fusion.64, f32[]{:T(128)} %bitcast.112, bf16[96,2560]{1,0:T(8,128)(2,1)S(1)} %get-tuple-element.547), kind=kOutput, calls=%fused_computation.6.clone.1 | convolution fusion | flops 25444352 | bytes 1492480 | tf_op jit(solution)/shard_map/while/body/eval_jaxpr/dot_general | solution.py:74
  99.6 1.7 constant_dynamic-slice_fusion.11
  105.7 2.8 %fusion.66 = f32[512,2560]{1,0:T(8,128)} fusion(f32[512,2560]{1,0:T(8,128)} %get-tuple-element.520, s32[]{:T(128)S(6)} %select_n.197, f32[96,512]{1,0:T(8,128)S(1)} %get-tuple-element.495, f32[96,512]{1,0:T(8,128)S(1)} %fusion.64, f32[]{:T(128)} %bitcast.112, bf16[96,2560]{1,0:T(8,128)(2,1)S(1)} %get-tuple-element.547), kind=kOutput, calls=%fused_computation.6.clone.1 | convolution fusion | flops 25444352 | bytes 1492480 | tf_op jit(solution)/shard_map/while/body/eval_jaxpr/dot_general | solution.py:74
  111.9 1.7 constant_dynamic-slice_fusion.11
  118.0 2.9 %fusion.66 = f32[512,2560]{1,0:T(8,128)} fusion(f32[512,2560]{1,0:T(8,128)} %get-tuple-element.520, s32[]{:T(128)S(6)} %select_n.197, f32[96,512]{1,0:T(8,128)S(1)} %get-tuple-element.495, f32[96,512]{1,0:T(8,128)S(1)} %fusion.64, f32[]{:T(128)} %bitcast.112, bf16[96,2560]{1,0:T(8,128)(2,1)S(1)} %get-tuple-element.547), kind=kOutput, calls=%fused_computation.6.clone.1 | convolution fusion | flops 25444352 | bytes 1492480 | tf_op jit(solution)/shard_map/while/body/eval_jaxpr/dot_general | solution.py:74
  124.3 1.6 constant_dynamic-slice_fusion.11
  130.3 2.8 %fusion.66 = f32[512,2560]{1,0:T(8,128)} fusion(f32[512,2560]{1,0:T(8,128)} %get-tuple-element.520, s32[]{:T(128)S(6)} %select_n.197, f32[96,512]{1,0:T(8,128)S(1)} %get-tuple-element.495, f32[96,512]{1,0:T(8,128)S(1)} %fusion.64, f32[]{:T(128)} %bitcast.112, bf16[96,2560]{1,0:T(8,128)(2,1)S(1)} %get-tuple-element.547), kind=kOutput, calls=%fused_computation.6.clone.1 | convolution fusion | flops 25444352 | bytes 1492480 | tf_op jit(solution)/shard_map/while/body/eval_jaxpr/dot_general | solution.py:74
  136.5 1.7 constant_dynamic-slice_fusion.11
  142.5 2.8 %fusion.66 = f32[512,2560]{1,0:T(8,128)} fusion(f32[512,2560]{1,0:T(8,128)} %get-tuple-element.520, s32[]{:T(128)S(6)} %select_n.197, f32[96,512]{1,0:T(8,128)S(1)} %get-tuple-element.495, f32[96,512]{1,0:T(8,128)S(1)} %fusion.64, f32[]{:T(128)} %bitcast.112, bf16[96,2560]{1,0:T(8,128)(2,1)S(1)} %get-tuple-element.547), kind=kOutput, calls=%fused_computation.6.clone.1 | convolution fusion | flops 25444352 | bytes 1492480 | tf_op jit(solution)/shard_map/while/body/eval_jaxpr/dot_general | solution.py:74
  148.7 1.7 constant_dynamic-slice_fusion.11
  154.8 2.8 %fusion.66 = f32[512,2560]{1,0:T(8,128)} fusion(f32[512,2560]{1,0:T(8,128)} %get-tuple-element.520, s32[]{:T(128)S(6)} %select_n.197, f32[96,512]{1,0:T(8,128)S(1)} %get-tuple-element.495, f32[96,512]{1,0:T(8,128)S(1)} %fusion.64, f32[]{:T(128)} %bitcast.112, bf16[96,2560]{1,0:T(8,128)(2,1)S(1)} %get-tuple-element.547), kind=kOutput, calls=%fused_computation.6.clone.1 | convolution fusion | flops 25444352 | bytes 1492480 | tf_op jit(solution)/shard_map/while/body/eval_jaxpr/dot_general | solution.py:74
  161.0 1.7 constant_dynamic-slice_fusion.11
  167.2 2.8 %fusion.66 = f32[512,2560]{1,0:T(8,128)} fusion(f32[512,2560]{1,0:T(8,128)} %get-tuple-element.520, s32[]{:T(128)S(6)} %select_n.197, f32[96,512]{1,0:T(8,128)S(1)} %get-tuple-element.495, f32[96,512]{1,0:T(8,128)S(1)} %fusion.64, f32[]{:T(128)} %bitcast.112, bf16[96,2560]{1,0:T(8,128)(2,1)S(1)} %get-tuple-element.547), kind=kOutput, calls=%fused_computation.6.clone.1 | convolution fusion | flops 25444352 | bytes 1492480 | tf_op jit(solution)/shard_map/while/body/eval_jaxpr/dot_general | solution.py:74
  173.4 1.7 constant_dynamic-slice_fusion.11
  179.5 2.8 %fusion.66 = f32[512,2560]{1,0:T(8,128)} fusion(f32[512,2560]{1,0:T(8,128)} %get-tuple-element.520, s32[]{:T(128)S(6)} %select_n.197, f32[96,512]{1,0:T(8,128)S(1)} %get-tuple-element.495, f32[96,512]{1,0:T(8,128)S(1)} %fusion.64, f32[]{:T(128)} %bitcast.112, bf16[96,2560]{1,0:T(8,128)(2,1)S(1)} %get-tuple-element.547), kind=kOutput, calls=%fused_computation.6.clone.1 | convolution fusion | flops 25444352 | bytes 1492480 | tf_op jit(solution)/shard_map/while/body/eval_jaxpr/dot_general | solution.py:74
  191.8 2.8 %fusion.66 = f32[512,2560]{1,0:T(8,128)} fusion(f32[512,2560]{1,0:T(8,128)} %get-tuple-element.520, s32[]{:T(128)S(6)} %select_n.197, f32[96,512]{1,0:T(8,128)S(1)} %get-tuple-element.495, f32[96,512]{1,0:T(8,128)S(1)} %fusion.64, f32[]{:T(128)} %bitcast.112, bf16[96,2560]{1,0:T(8,128)(2,1)S(1)} %get-tuple-element.547), kind=kOutput, calls=%fused_computation.6.clone.1 | convolution fusion | flops 25444352 | bytes 1492480 | tf_op jit(solution)/shard_map/while/body/eval_jaxpr/dot_general | solution.py:74
  194.5 4.6 %all-to-all-start.2 = ((f32[96,2,1280]{2,1,0:T(2,128)}), f32[96,2,1280]{2,1,0:T(2,128)S(1)}, u32[]{:S(2)}, u32[]{:S(2)}) async-start(f32[96,2,1280]{2,1,0:T(2,128)} %get-tuple-element.205), calls=%async_computation.2 | async-start | bytes 1966080 | tf_op jit(solution)/shard_map/all_to_all | solution.py:184
  199.3 5.9 %convert_element_type.46 = bf16[512,2,1280]{2,1,0:T(2,128)(2,1)} convert(f32[512,2,1280]{2,1,0:T(2,128)} %get-tuple-element.206) | non-fusion elementwise | flops 1310720 | bytes 7864320 | tf_op jit(solution)/shard_map/convert_element_type | solution.py:192
  205.3 1.8 convert_element_type.47
  207.1 15.7 %all-to-all-done.2 = f32[96,2,1280]{2,1,0:T(2,128)S(1)} async-done(((f32[96,2,1280]{2,1,0:T(2,128)}), f32[96,2,1280]{2,1,0:T(2,128)S(1)}, u32[]{:S(2)}, u32[]{:S(2)}) %all-to-all-start.2) | async-done | bytes 983072 | tf_op jit(solution)/shard_map/all_to_all | solution.py:184
  (268 shorter events, 91.5 us)
Async XLA Ops:
  0.6 15.7 %copy-start = (bf16[8,2,1280]{2,1,0:T(2,128)(2,1)S(1)}, bf16[8,2,1280]{2,1,0:T(2,128)(2,1)}, u32[]{:S(2)}) copy-start(bf16[8,2,1280]{2,1,0:T(2,128)(2,1)} %param.14) | copy-start | bytes 122884
  0.6 17.3 %copy-start.4 = (s32[16]{0:T(128)S(1)}, s32[16]{0:T(128)}, u32[]{:S(2)}) copy-start(s32[16]{0:T(128)} %param.22) | copy-start | bytes 196
  0.7 15.2 %copy-start.3 = (s32[16,12]{1,0:T(8,128)S(1)}, s32[16,12]{1,0:T(8,128)}, u32[]{:S(2)}) copy-start(s32[16,12]{1,0:T(8,128)} %param.21) | copy-start | bytes 2308
  0.7 15.6 %copy-start.1 = (bf16[8,2560]{1,0:T(8,128)(2,1)S(1)}, bf16[8,2560]{1,0:T(8,128)(2,1)}, u32[]{:S(2)}) copy-start(bf16[8,2560]{1,0:T(8,128)(2,1)} %param.18) | copy-start | bytes 122884
  0.7 15.5 %copy-start.5 = (f32[10]{0:T(128)S(1)}, f32[10]{0:T(128)}, u32[]{:S(2)}) copy-start(f32[10]{0:T(128)} %param.20) | copy-start | bytes 124
  0.7 15.6 %copy-start.2 = (bf16[8,2,2560]{2,1,0:T(2,128)(2,1)S(1)}, bf16[8,2,2560]{2,1,0:T(2,128)(2,1)}, u32[]{:S(2)}) copy-start(bf16[8,2,2560]{2,1,0:T(2,128)(2,1)} %param.17) | copy-start | bytes 245764
  1.5 18.1 %collective-permute-start = (f32[8,2,10]{0,1,2:T(2,128)S(1)}, f32[8,2,10]{0,1,2:T(2,128)S(1)}, u32[]{:S(2)}, u32[]{:S(2)}) collective-permute-start(f32[8,2,10]{0,1,2:T(2,128)S(1)} %copy.65), channel_id=1, source_target_pairs={{0,1},{1,0},{2,3},{3,2},{4,5},{5,4},{6,7},{7,6},{8,9},{9,8},{10,11... | collective-permute-start | bytes 1928 | tf_op jit(solution)/shard_map/ppermute | solution.py:11
  9.9 22.9 %all-to-all-start.1 = ((bf16[16,6,2560]{2,1,0:T(8,128)(2,1)}), bf16[16,6,2560]{2,1,0:T(8,128)(2,1)S(1)}, u32[]{:S(2)}, u32[]{:S(2)}) async-start(bf16[16,6,2560]{2,1,0:T(8,128)(2,1)} %broadcast_select_fusion.1), calls=%async_computation.1 | async-start | bytes 1310720 | tf_op jit(solution)/shard_map/all_to_all | solution.py:167
  19.7 3.2 %collective-permute-start.1 = (f32[16,2,10]{0,1,2:T(2,128)S(1)}, f32[16,2,10]{0,1,2:T(2,128)S(1)}, u32[]{:S(2)}, u32[]{:S(2)}) collective-permute-start(f32[16,2,10]{0,1,2:T(2,128)S(1)} %maximum_select_fusion), channel_id=1, source_target_pairs={{0,2},{1,3},{2,0},{3,1},{4,6},{5,7},{6,4},{7,5},{8,10},{9,11},{10,... | collective-permute-start | bytes 3848 | tf_op jit(solution)/shard_map/ppermute | solution.py:11
  23.0 14.3 %collective-permute-start.2 = (f32[32,2,10]{0,1,2:T(2,128)S(1)}, f32[32,2,10]{0,1,2:T(2,128)S(1)}, u32[]{:S(2)}, u32[]{:S(2)}) collective-permute-start(f32[32,2,10]{0,1,2:T(2,128)S(1)} %maximum_select_fusion.1), channel_id=1, source_target_pairs={{0,4},{1,5},{2,6},{3,7},{4,0},{5,1},{6,2},{7,3},{8,12},{9,13},{10,... | collective-permute-start | bytes 7688 | tf_op jit(solution)/shard_map/ppermute | solution.py:11
  32.8 30.9 %all-to-all-start = ((bf16[96,2,1280]{2,1,0:T(2,128)(2,1)}), bf16[96,2,1280]{2,1,0:T(2,128)(2,1)S(1)}, u32[]{:S(2)}, u32[]{:S(2)}) async-start(bf16[96,2,1280]{2,1,0:T(2,128)(2,1)} %broadcast_select_fusion), calls=%async_computation | async-start | bytes 983040 | tf_op jit(solution)/shard_map/all_to_all | solution.py:166
  37.4 24.7 %collective-permute-start.3 = (f32[64,2,10]{0,1,2:T(2,128)S(1)}, f32[64,2,10]{0,1,2:T(2,128)S(1)}, u32[]{:S(2)}, u32[]{:S(2)}) collective-permute-start(f32[64,2,10]{0,1,2:T(2,128)S(1)} %maximum_select_fusion.2), channel_id=1, source_target_pairs={{0,8},{1,9},{2,10},{3,11},{4,12},{5,13},{6,14},{7,15},{8,0},{9,1},... | collective-permute-start | bytes 15368 | tf_op jit(solution)/shard_map/ppermute | solution.py:11
  194.5 10.7 %slice-start = ((s8[5242880]{0:T(1024)(128)(4,1)}), s8[1048576]{0:T(1024)(128)(4,1)S(1)}, s32[]{:S(2)}) async-start(s8[5242880]{0:T(1024)(128)(4,1)} %bitcast.115), calls=%async_computation.3 | async-start | bytes 2097152
  194.5 28.2 %all-to-all-start.2 = ((f32[96,2,1280]{2,1,0:T(2,128)}), f32[96,2,1280]{2,1,0:T(2,128)S(1)}, u32[]{:S(2)}, u32[]{:S(2)}) async-start(f32[96,2,1280]{2,1,0:T(2,128)} %get-tuple-element.205), calls=%async_computation.2 | async-start | bytes 1966080 | tf_op jit(solution)/shard_map/all_to_all | solution.py:184
  199.3 5.9 %slice-start.1 = ((s8[5242880]{0:T(1024)(128)(4,1)}), s8[4194304]{0:T(1024)(128)(4,1)S(1)}, s32[]{:S(2)}) async-start(s8[5242880]{0:T(1024)(128)(4,1)} %bitcast.115), calls=%async_computation.4 | async-start | bytes 8388608
